TPU v7x, 32 devices: a whole 2x2x4 slice. The times are simulated.
32 devices in a mesh: dp: 4 (over y, x), seq: 8 (over z, core).
Axes of the slice: x: 2, y: 2, z: 4, core: 2. Of those that a mesh axis runs over, the one named last changes fastest.
Arguments:
- tiles: bfloat16 [4, 8192, 768], P('dp', 'seq'), may hold values from -48 to 48
- tile_count: int32 [4], P('dp'), may hold values from 4097 to 8192
- offsets: int32 [16], replicated, may hold values from 0 to 15
- w_query: bfloat16 [768, 768], replicated, may hold values from -0.375 to 0.375
- w_key: bfloat16 [768, 768], replicated, may hold values from -0.375 to 0.375
- w_value: bfloat16 [768, 768], replicated, may hold values from -0.21875 to 0.21875
- w_out: bfloat16 [768, 768], replicated, may hold values from -0.21875 to 0.21875
- cotangent: bfloat16 [4, 8192, 768], P('dp', 'seq'), may hold values from -0.046875 to 0.046875
Outputs:
- branch: bfloat16 [4, 8192, 768], P('dp', 'seq')
- grad_out: float32 [768, 768], P(None, 'seq')
All inputs are finite; a program needn't handle non-finite values.
Results may differ from a plain program's by a relative error of at most 0.0095.
The roundings to bfloat16 on the way count: a program that leaves them out, or rounds other values in their place, can miss the bound.
Values may be sent and summed in bfloat16 or wider, within the bound.
A program may use at most 128 MiB of HBM per device.

v0:
```python
import jax
import jax.numpy as jnp
from jax import lax
from jax.sharding import PartitionSpec as P

D = 768
ATTENTION_HEADS = 16
HEAD_SIZE = 48
SEG = 1024
RATE = 16


NEGATIVE_FLOOR = -1e30
head_group = 4


def project(inputs, weight):
    return jnp.dot(inputs, weight, preferred_element_type=jnp.float32).astype(jnp.bfloat16)


def select_rows(tensor, offsets):
    segment_height = tensor.shape[0]
    grouped = tensor.reshape(segment_height // RATE, RATE, ATTENTION_HEADS, HEAD_SIZE)
    onehot = (jnp.arange(RATE, dtype=jnp.int32)[:, None] == offsets[None, :]).astype(jnp.bfloat16)
    return jnp.einsum("arhd,rh->ahd", grouped, onehot, preferred_element_type=jnp.float32).astype(
        jnp.bfloat16
    )


def local_attention(query_proj, key_proj, value_proj, is_live):
    segment_height = query_proj.shape[0]
    segments = segment_height // SEG
    groups = ATTENTION_HEADS // head_group
    query_seg = query_proj.reshape(segments, SEG, groups, head_group, HEAD_SIZE)
    key_seg = key_proj.reshape(segments, SEG, groups, head_group, HEAD_SIZE)
    value_seg = value_proj.reshape(segments, SEG, groups, head_group, HEAD_SIZE)
    alive_seg = is_live.reshape(segments, SEG)

    def one_group(index):
        query_part = lax.dynamic_index_in_dim(query_seg, index, 2, keepdims=False)
        key_part = lax.dynamic_index_in_dim(key_seg, index, 2, keepdims=False)
        value_part = lax.dynamic_index_in_dim(value_seg, index, 2, keepdims=False)
        scores = jnp.einsum(
            "sqhd,skhd->shqk", query_part, key_part, preferred_element_type=jnp.float32
        ) * HEAD_SIZE ** (-0.5)
        scores = jnp.where(alive_seg[:, None, None, :], scores, NEGATIVE_FLOOR)
        maxima = jnp.max(scores, axis=-1)
        weights = jnp.exp(scores - maxima[..., None])
        totals = jnp.sum(weights, axis=-1)
        weighted = jnp.einsum(
            "shqk,skhd->sqhd",
            weights.astype(jnp.bfloat16),
            value_part,
            preferred_element_type=jnp.float32,
        )
        return (maxima, totals, weighted)

    maxima, totals, weighted = lax.map(one_group, jnp.arange(groups, dtype=jnp.int32))
    maxima = maxima.transpose(1, 3, 0, 2).reshape(segment_height, ATTENTION_HEADS)
    totals = totals.transpose(1, 3, 0, 2).reshape(segment_height, ATTENTION_HEADS)
    weighted = weighted.transpose(1, 2, 0, 3, 4).reshape(segment_height, ATTENTION_HEADS, HEAD_SIZE)
    return (maxima, totals, weighted)


def combine(local, dilated_branch, offsets, is_live):
    local_max, local_total, local_sum = local
    dilated_row_max, dilated_value_total, dilated_row_sum = dilated_branch
    segment_height = local_max.shape[0]
    dilation_match = jnp.arange(RATE, dtype=jnp.int32)[:, None] == offsets[None, :]
    dense_row_max = jnp.where(
        dilation_match[None], dilated_row_max[:, None, :], NEGATIVE_FLOOR
    ).reshape(segment_height, ATTENTION_HEADS)
    dense_value_total = jnp.where(
        dilation_match[None], dilated_value_total[:, None, :], 0.0
    ).reshape(segment_height, ATTENTION_HEADS)
    dense_row_sum = jnp.where(
        dilation_match[None, :, :, None], dilated_row_sum[:, None], 0.0
    ).reshape(segment_height, ATTENTION_HEADS, HEAD_SIZE)
    top = jnp.maximum(local_max, dense_row_max)
    near = jnp.exp(local_max - top)
    far = jnp.exp(dense_row_max - top)
    attn = (near[..., None] * local_sum + far[..., None] * dense_row_sum) / (
        near * local_total + far * dense_value_total
    )[..., None]
    attn = jnp.where(is_live[:, None, None], attn, 0.0)
    return attn.reshape(segment_height, D).astype(jnp.bfloat16)


def body(tiles, tile_count, offsets, w_query, w_key, w_value, w_out, cotangent):
    inputs = tiles[0]
    segment_height = inputs.shape[0]
    shard_rank = lax.axis_index("seq")
    live_count = tile_count[0]
    query_proj = project(inputs, w_query).reshape(segment_height, ATTENTION_HEADS, HEAD_SIZE)
    key_proj = project(inputs, w_key).reshape(segment_height, ATTENTION_HEADS, HEAD_SIZE)
    value_proj = project(inputs, w_value).reshape(segment_height, ATTENTION_HEADS, HEAD_SIZE)
    positions = shard_rank * segment_height + jnp.arange(segment_height, dtype=jnp.int32)
    is_live = positions < live_count
    local = local_attention(query_proj, key_proj, value_proj, is_live)
    picked = segment_height // RATE
    query_sel = select_rows(query_proj, offsets)
    key_sel = select_rows(key_proj, offsets)
    value_sel = select_rows(value_proj, offsets)
    score_scale = HEAD_SIZE ** (-0.5)
    portion = (
        lax.all_gather(key_sel.reshape(picked, D), "seq", axis=0, tiled=True),
        lax.all_gather(value_sel.reshape(picked, D), "seq", axis=0, tiled=True),
    )
    old_max = jnp.full((picked, ATTENTION_HEADS), NEGATIVE_FLOOR, jnp.float32)
    key_part = portion[0].reshape(portion[0].shape[0], ATTENTION_HEADS, HEAD_SIZE)
    value_part = portion[1].reshape(portion[1].shape[0], ATTENTION_HEADS, HEAD_SIZE)
    amount = key_part.shape[0]
    key_live = jnp.arange(amount, dtype=jnp.int32)[:, None] * RATE + offsets[None, :] < live_count
    scores = (
        jnp.einsum("qhd,khd->qhk", query_sel, key_part, preferred_element_type=jnp.float32)
        * score_scale
    )
    scores = jnp.where(key_live.T[None], scores, NEGATIVE_FLOOR)
    new_max = jnp.maximum(old_max, jnp.max(scores, axis=-1))
    weights = jnp.exp(scores - new_max[..., None])
    new_total = jnp.sum(weights, axis=-1)
    new_sum = jnp.einsum(
        "qhk,khd->qhd", weights.astype(jnp.bfloat16), value_part, preferred_element_type=jnp.float32
    )
    dilated_branch = (new_max, new_total, new_sum)
    attn = combine(local, dilated_branch, offsets, is_live)
    branch = jnp.dot(attn, w_out, preferred_element_type=jnp.float32).astype(jnp.bfloat16)[None]
    gradient_in = cotangent[0]
    shares = lax.psum_scatter(
        jnp.einsum("tc,td->cd", gradient_in, attn, preferred_element_type=jnp.float32),
        "seq",
        scatter_dimension=0,
        tiled=True,
    )
    grad_part = lax.psum(shares.astype(jnp.bfloat16), "dp").astype(jnp.float32).T
    return (branch, grad_part)


def solution(mesh):
    in_specs = (P("dp", "seq", None), P("dp"), P(), P(), P(), P(), P(), P("dp", "seq", None))
    out_specs = (P("dp", "seq", None), P(None, "seq"))
    return jax.shard_map(body, mesh=mesh, in_specs=in_specs, out_specs=out_specs, check_vma=False)
```

profile of v0, /device:TPU:0, one launch (start us, length us, event | category | flops | bytes accessed | tf_op | source)
XLA Modules:
  0.0 290.6 jit_solution(8163011718679875207)
XLA Ops:
  23.6 7.2 %reshape_reshape.22 = bf16[64,16,16,48]{3,2,1,0:T(8,128)(2,1)} reshape(bf16[1024,768]{1,0:T(8,128)(2,1)} %copy.47) | data formatting | bytes 3145728 | tf_op jit(solution)/shard_map/reshape;reshape | solution.py:23
  30.8 7.2 %reshape_reshape.21 = bf16[64,16,16,48]{3,2,1,0:T(8,128)(2,1)} reshape(bf16[1024,768]{1,0:T(8,128)(2,1)} %copy.45) | data formatting | bytes 3145728 | tf_op jit(solution)/shard_map/reshape;reshape | solution.py:23
  38.0 7.2 %reshape_reshape.23 = bf16[64,16,16,48]{3,2,1,0:T(8,128)(2,1)} reshape(bf16[1024,768]{1,0:T(8,128)(2,1)} %copy.49) | data formatting | bytes 3145728 | tf_op jit(solution)/shard_map/reshape;reshape | solution.py:23
  45.2 9.0 %multiply_reduce_fusion.1 = (bf16[16,64,48]{2,0,1:T(8,128)(2,1)S(1)}, bf16[16,64,48]{2,0,1:T(8,128)(2,1)}, bf16[16,64,48]{2,0,1:T(8,128)(2,1)}) fusion(f32[16,16]{0,1:T(8,128)S(1)} %copy.80, bf16[64,16,16,48]{3,2,1,0:T(8,128)(2,1)} %reshape_reshape.22, bf16[64,16,16,48]{3,2,1,0:T(8,128)(2,1)} %reshape_reshape.23, bf16[64,16,16,48]{3,2,1,0:T(8,128)(2,1)} %reshape_reshape.21), kind=kLoop, calls=%fused_computation.25 | loop fusion | flops 6930432 | bytes 5014528
  57.5 18.4 %all_gather.6 = bf16[512,768]{1,0:T(8,128)(2,1)} all-gather(bf16[64,768]{1,0:T(8,128)(2,1)S(1)} %reshape.263), channel_id=1, replica_groups=mesh['dp'=4,'seq'=8] {'seq'}, dimensions={0}, use_global_device_ids=true | all-gather | bytes 884736 | tf_op jit(solution)/shard_map/all_gather | solution.py:106
  78.3 16.6 %all_gather.7 = bf16[512,768]{1,0:T(8,128)(2,1)} all-gather(bf16[64,768]{1,0:T(8,128)(2,1)S(1)} %reshape.266), channel_id=1, replica_groups=mesh['dp'=4,'seq'=8] {'seq'}, dimensions={0}, use_global_device_ids=true | all-gather | bytes 884736 | tf_op jit(solution)/shard_map/all_gather | solution.py:107
  108.7 66.5 %while.15 = (s32[]{:T(128)}, f32[4,1,4,1024]{3,2,1,0:T(4,128)}, f32[4,1,4,1024]{3,2,1,0:T(4,128)}, f32[4,1,1024,4,48]{2,4,3,1,0:T(8,128)}, s32[4]{0:T(128)S(1)},...) while((s32[]{:T(128)}, f32[4,1,4,1024]{3,2,1,0:T(4,128)}, ...), condition=%wide.region_3.4_spmd.clone, body=%wide.region_0.3_spmd.clone.sunk | while | flops 851437568 | bytes 52434116 | solution.py:58
  115.0 4.1 %fusion.71 = f32[4,1024]{1,0:T(4,128)S(1)} fusion(f32[4,1024,1024]{1,2,0:T(8,128)S(1)} %get-tuple-element.187, f32[4,1024]{1,0:T(4,128)S(1)} %get-tuple-element.188, pred[1024]{0:T(1024)(128)(4,1)S(1)} %add_compare_fusion.4), kind=kLoop, calls=%fused_computation.5.clone.1 | loop fusion | flops 16773120 | bytes 16811008 | tf_op jit(solution)/shard_map/while/body/eval_jaxpr/reduce_sum | solution.py:49
  119.1 5.7 %fusion.72 = f32[4,1,1024,4,48]{2,4,3,1,0:T(8,128)} fusion(f32[4,1,1024,4,48]{2,4,3,1,0:T(8,128)} %get-tuple-element.207, s32[]{:T(128)S(6)} %copy.89, f32[4,1024,1024]{1,2,0:T(8,128)S(1)} %get-tuple-element.187, f32[4,1024]{1,0:T(4,128)S(1)} %get-tuple-element.188, pred[1024]{0:T(1024)(128)(4,1)S(1)} %add_compare_fusion.4, ...), kind=kOutput, calls=%fused_computation.9.clone.1 | convolution fusion | flops 419430400 | bytes 17974280 | tf_op jit(solution)/shard_map/while/body/eval_jaxpr/shqk,skhd->sqhd/dot_general | solution.py:50
  131.6 4.1 %fusion.71 = f32[4,1024]{1,0:T(4,128)S(1)} fusion(f32[4,1024,1024]{1,2,0:T(8,128)S(1)} %get-tuple-element.187, f32[4,1024]{1,0:T(4,128)S(1)} %get-tuple-element.188, pred[1024]{0:T(1024)(128)(4,1)S(1)} %add_compare_fusion.4), kind=kLoop, calls=%fused_computation.5.clone.1 | loop fusion | flops 16773120 | bytes 16811008 | tf_op jit(solution)/shard_map/while/body/eval_jaxpr/reduce_sum | solution.py:49
  135.8 5.6 %fusion.72 = f32[4,1,1024,4,48]{2,4,3,1,0:T(8,128)} fusion(f32[4,1,1024,4,48]{2,4,3,1,0:T(8,128)} %get-tuple-element.207, s32[]{:T(128)S(6)} %copy.89, f32[4,1024,1024]{1,2,0:T(8,128)S(1)} %get-tuple-element.187, f32[4,1024]{1,0:T(4,128)S(1)} %get-tuple-element.188, pred[1024]{0:T(1024)(128)(4,1)S(1)} %add_compare_fusion.4, ...), kind=kOutput, calls=%fused_computation.9.clone.1 | convolution fusion | flops 419430400 | bytes 17974280 | tf_op jit(solution)/shard_map/while/body/eval_jaxpr/shqk,skhd->sqhd/dot_general | solution.py:50
  148.3 4.1 %fusion.71 = f32[4,1024]{1,0:T(4,128)S(1)} fusion(f32[4,1024,1024]{1,2,0:T(8,128)S(1)} %get-tuple-element.187, f32[4,1024]{1,0:T(4,128)S(1)} %get-tuple-element.188, pred[1024]{0:T(1024)(128)(4,1)S(1)} %add_compare_fusion.4), kind=kLoop, calls=%fused_computation.5.clone.1 | loop fusion | flops 16773120 | bytes 16811008 | tf_op jit(solution)/shard_map/while/body/eval_jaxpr/reduce_sum | solution.py:49
  152.4 5.6 %fusion.72 = f32[4,1,1024,4,48]{2,4,3,1,0:T(8,128)} fusion(f32[4,1,1024,4,48]{2,4,3,1,0:T(8,128)} %get-tuple-element.207, s32[]{:T(128)S(6)} %copy.89, f32[4,1024,1024]{1,2,0:T(8,128)S(1)} %get-tuple-element.187, f32[4,1024]{1,0:T(4,128)S(1)} %get-tuple-element.188, pred[1024]{0:T(1024)(128)(4,1)S(1)} %add_compare_fusion.4, ...), kind=kOutput, calls=%fused_computation.9.clone.1 | convolution fusion | flops 419430400 | bytes 17974280 | tf_op jit(solution)/shard_map/while/body/eval_jaxpr/shqk,skhd->sqhd/dot_general | solution.py:50
  164.9 4.1 %fusion.71 = f32[4,1024]{1,0:T(4,128)S(1)} fusion(f32[4,1024,1024]{1,2,0:T(8,128)S(1)} %get-tuple-element.187, f32[4,1024]{1,0:T(4,128)S(1)} %get-tuple-element.188, pred[1024]{0:T(1024)(128)(4,1)S(1)} %add_compare_fusion.4), kind=kLoop, calls=%fused_computation.5.clone.1 | loop fusion | flops 16773120 | bytes 16811008 | tf_op jit(solution)/shard_map/while/body/eval_jaxpr/reduce_sum | solution.py:49
  169.0 5.6 %fusion.72 = f32[4,1,1024,4,48]{2,4,3,1,0:T(8,128)} fusion(f32[4,1,1024,4,48]{2,4,3,1,0:T(8,128)} %get-tuple-element.207, s32[]{:T(128)S(6)} %copy.89, f32[4,1024,1024]{1,2,0:T(8,128)S(1)} %get-tuple-element.187, f32[4,1024]{1,0:T(4,128)S(1)} %get-tuple-element.188, pred[1024]{0:T(1024)(128)(4,1)S(1)} %add_compare_fusion.4, ...), kind=kOutput, calls=%fused_computation.9.clone.1 | convolution fusion | flops 419430400 | bytes 17974280 | tf_op jit(solution)/shard_map/while/body/eval_jaxpr/shqk,skhd->sqhd/dot_general | solution.py:50
  176.9 4.9 %broadcast_in_dim.156 = f32[64,16,16,48]{3,2,1,0:T(8,128)} broadcast(f32[64,16,48]{2,1,0:T(8,128)} %copy.51), dimensions={0,2,3} | broadcast | bytes 3342336 | tf_op jit(solution)/shard_map/jit(_where)/broadcast_in_dim | solution.py:76
  181.9 6.6 %copy.53 = f32[1024,16,48]{0,2,1:T(8,128)} copy(f32[1024,16,48]{2,1,0:T(8,128)} %bitcast.162) | data formatting | bytes 6291456 | tf_op jit(solution)/shard_map/jit(_where)/broadcast_in_dim | solution.py:76
  188.5 4.0 %fusion.32 = bf16[1024,16,48]{0,2,1:T(8,128)(2,1)S(1)} fusion(f32[1024,16,48]{0,2,1:T(8,128)} %copy.53, f32[4,1,1024,4,48]{2,4,3,1,0:T(8,128)} %get-tuple-element.52, f32[1024,16]{0,1:T(8,128)S(1)} %get-tuple-element.111, f32[1024,16]{0,1:T(8,128)S(1)} %get-tuple-element.113, f32[1024,16]{0,1:T(8,128)S(1)} %get-tuple-element.112, ...), kind=kLoop, calls=%fused_computation.37 | loop fusion | flops 5505024 | bytes 8078336 | tf_op jit(solution)/shard_map/convert_element_type | solution.py:86
  198.5 7.9 %broadcast_in_dim.157 = f32[1024,768]{1,0:T(8,128)} reshape(f32[64,16,16,48]{3,2,1,0:T(8,128)} %broadcast_in_dim.156) | data formatting | bytes 6291456 | tf_op jit(solution)/shard_map/jit(_where)/broadcast_in_dim | solution.py:76
  206.5 3.6 %copy.52 = f32[1024,768]{0,1:T(8,128)} copy(f32[1024,768]{1,0:T(8,128)} %broadcast_in_dim.157) | data formatting | bytes 6291456 | tf_op jit(solution)/shard_map/jit(_where)/broadcast_in_dim | solution.py:76
  210.0 3.9 %fusion.31 = bf16[1024,768]{0,1:T(8,128)(2,1)S(1)} fusion(f32[1024,768]{0,1:T(8,128)} %copy.52, f32[4,1,1024,4,48]{2,4,3,1,0:T(8,128)} %get-tuple-element.52, f32[1024,16]{0,1:T(8,128)S(1)} %get-tuple-element.111, f32[1024,16]{0,1:T(8,128)S(1)} %get-tuple-element.113, f32[1024,16]{0,1:T(8,128)S(1)} %get-tuple-element.112, ...), kind=kLoop, calls=%fused_computation.36 | loop fusion | flops 5505024 | bytes 8078336 | tf_op jit(solution)/shard_map/convert_element_type | solution.py:86
  213.9 23.1 %reduce-scatter.4.cloned.1.call-done = f32[96,768]{1,0:T(8,128)} async-done(((f32[768,768]{1,0:T(8,128)}), f32[96,768]{1,0:T(8,128)}) %reduce-scatter.4.cloned.1.call-update) | async-done | bytes 294928
  238.8 4.0 %fusion.40 = bf16[1,1024,768]{2,1,0:T(8,128)(2,1)} fusion(bf16[1024,768]{0,1:T(8,128)(2,1)S(1)} %fusion.31, bf16[768,768]{1,0:T(8,128)(2,1)} %param.16), kind=kOutput, calls=%fused_computation.53 | convolution fusion | flops 1208745984 | bytes 4325376 | tf_op jit(solution)/shard_map/dot_general | solution.py:127
  242.7 39.3 %all-reduce.2.cloned.1.call-done = bf16[768,96]{1,0:T(8,128)(2,1)} async-done(((bf16[768,96]{1,0:T(8,128)(2,1)}), bf16[768,96]{1,0:T(8,128)(2,1)}) %all-reduce.2.cloned.1.call-update) | async-done | bytes 147472 | tf_op jit(solution)/shard_map/psum | solution.py:135
  (84 shorter events, 67.3 us)
Async XLA Ops:
  7.2 2.5 copy-start
  7.2 229.8 %reduce-scatter.4.cloned.1.call-start = ((), (), s32[]{:S(2)}) async-start(), calls=%async_computation.2 | async-start | bytes 2654208
  9.6 2.8 copy-start.11
  12.5 2.6 copy-start.12
  17.7 2.8 copy-start.2
  57.5 39.7 %copy-start.3 = (bf16[16,64,48]{1,2,0:T(8,128)(2,1)S(1)}, bf16[16,64,48]{1,2,0:T(8,128)(2,1)}, u32[]{:S(2)}) copy-start(bf16[16,64,48]{1,2,0:T(8,128)(2,1)} %copy.70) | copy-start | bytes 294916
  76.0 21.2 %copy-start.8 = (s32[512]{0:T(512)S(1)}, s32[512]{0:T(512)}, u32[]{:S(2)}) copy-start(s32[512]{0:T(512)} %iota_multiply_fusion) | copy-start | bytes 6148
  76.0 21.2 %copy-start.9 = (s32[16]{0:T(128)S(1)}, s32[16]{0:T(128)}, u32[]{:S(2)}) copy-start(s32[16]{0:T(128)} %param.12) | copy-start | bytes 196
  97.2 3.2 %copy-start.4 = (bf16[512,768]{0,1:T(8,128)(2,1)S(1)}, bf16[512,768]{0,1:T(8,128)(2,1)}, u32[]{:S(2)}) copy-start(bf16[512,768]{0,1:T(8,128)(2,1)} %copy.50) | copy-start | bytes 2359300
  99.1 1.4 copy-start.5
  181.9 6.6 %copy-start.6 = (pred[1024]{0:T(1024)(128)(4,1)S(1)}, pred[1024]{0:T(1024)(128)(4,1)}, u32[]{:S(2)}) copy-start(pred[1024]{0:T(1024)(128)(4,1)} %add_compare_fusion.2) | copy-start | bytes 3076
  188.5 4.0 %copy-start.10 = (bf16[1,1024,768]{2,1,0:T(8,128)(2,1)S(1)}, bf16[1,1024,768]{2,1,0:T(8,128)(2,1)}, u32[]{:S(2)}) copy-start(bf16[1,1024,768]{2,1,0:T(8,128)(2,1)} %param.17) | copy-start | bytes 4718596
  198.5 83.5 %all-reduce.2.cloned.1.call-start = ((), (), s32[]{:S(2)}) async-start(), calls=%async_computation.1 | async-start | bytes 393216 | tf_op jit(solution)/shard_map/psum | solution.py:135
  206.5 3.6 %copy-start.7 = (pred[1024]{0:T(1024)(128)(4,1)S(1)}, pred[1024]{0:T(1024)(128)(4,1)}, u32[]{:S(2)}) copy-start(pred[1024]{0:T(1024)(128)(4,1)} %add_compare_fusion.2) | copy-start | bytes 3076
  238.7 45.0 %copy-start.1 = (bf16[1,1024,768]{2,1,0:T(8,128)(2,1)S(1)}, bf16[1,1024,768]{2,1,0:T(8,128)(2,1)}, u32[]{:S(2)}) copy-start(bf16[1,1024,768]{2,1,0:T(8,128)(2,1)} %param.10) | copy-start | bytes 4718596
Sparse Core Ops, SparseCore 0:
  198.6 38.3 reduce-scatter.3
  240.4 41.5 all-reduce.1
where the time goes:
time: 292 us; the launch traced here: 291 us
  local copies, waits for them, and re-layouts  79 us (27%)
  waiting for transfers between devices  62.4 us (21%)
  matrix products  53.2 us (18%)
  other arithmetic  39.2 us (13%)
  blocking collectives  35 us (12%)
  between operations  14.9 us (5%)
  loops' own time  6.89 us (2%)
    psum x1, waiting for transfers between devices, body(): lax.psum(shares.astype(jnp.bfloat16), 'dp').astype(jnp.float32)  39.3 us
    unnamed x3, waiting for transfers between devices  23.1 us
    broadcast_in_dim x4, local copies, waits for them, and re-layouts, combine(): jnp.where(dilation_match[None, :, :, None], dilated_row_sum[:, None], 0.0)  23 us
    dot_general x4, matrix products, one_group(): jnp.einsum('shqk,skhd->sqhd', weights.astype(jnp.bfloat16), value_part, p...  22.5 us
    another operation x3, local copies, waits for them, and re-layouts, select_rows(): tensor.reshape(segment_height // RATE, RATE, ATTENTION_HEADS, HEAD_SIZE)  21.5 us
    all_gather x1, blocking collectives, body(): lax.all_gather(key_sel.reshape(picked, D), 'seq', axis=0, tiled=True)  18.4 us
    all_gather x1, blocking collectives, body(): lax.all_gather(value_sel.reshape(picked, D), 'seq', axis=0, tiled=True)  16.6 us
    reduce_sum x4, other arithmetic, one_group(): totals = jnp.sum(weights, axis=-1)  16.4 us
  transfers between devices with their start and end apart: 2, of which 2 were waited for; matrix products, arithmetic and copies ran while one was open for 7% of the time, Pallas kernels for 0%

commit v1 on v0

v1 whole, which is shorter than its diff:
```python
import functools

import jax
import jax.numpy as jnp
from jax import lax
from jax.experimental import pallas as pl
from jax.experimental.pallas import tpu as pltpu
from jax.sharding import PartitionSpec as P

ATTENTION_HEADS = 16
HEAD_SIZE = 48
SEG = 1024
RATE = 16
NEGATIVE_FLOOR = -1e30
LOG2_SCALE = 1.4426950408889634 / HEAD_SIZE**0.5
PAD = 16
BF16 = jnp.bfloat16
F32 = jnp.float32
VMEM = pl.BlockSpec(memory_space=pltpu.VMEM)
SMEM = pl.BlockSpec(memory_space=pltpu.SMEM)


def dot(a, b, ca=1, cb=0):
    return lax.dot_general(a, b, (((ca,), (cb,)), ((), ())), preferred_element_type=F32)


def head_rows(head):
    return pl.ds(pl.multiple_of(head * HEAD_SIZE, PAD), HEAD_SIZE)


def scaled_query(query):
    scaled = query.astype(F32) * LOG2_SCALE
    high = scaled.astype(BF16)
    low = (scaled - high.astype(F32)).astype(BF16)
    return jnp.concatenate([high, low, jnp.ones((PAD, query.shape[1]), BF16)], 0)


def masked_key(key, dead):
    row = lax.broadcasted_iota(jnp.int32, (PAD, key.shape[1]), 0)
    mask = jnp.where(dead & (row == 0), NEGATIVE_FLOOR, 0.0).astype(BF16)
    return jnp.concatenate([key, key, mask], 0)


def counted_value(value):
    return jnp.concatenate([value, jnp.ones((PAD, value.shape[1]), BF16)], 0)


def lanes(width):
    return lax.broadcasted_iota(jnp.int32, (PAD, width), 1)


def selector(length, offset):
    shape = (length, length // RATE)
    token = lax.broadcasted_iota(jnp.int32, shape, 0)
    pick = lax.broadcasted_iota(jnp.int32, shape, 1)
    return jnp.where(token == RATE * pick + offset, 1.0, 0.0).astype(BF16)


def project_kernel(offsets, x, wq, wk, wv, q_out, k_out, v_out, sel_out):
    length = x.shape[0]
    picked = length // RATE
    tiles = x[...]
    for weight, out in ((wk, k_out), (wv, v_out), (wq, q_out)):
        out[...] = dot(weight[...].T, tiles, 1, 1).astype(BF16)

    def pick(head, carry):
        rows = head_rows(head)
        onehot = selector(length, offsets[head])
        both = jnp.concatenate([k_out[rows, :], v_out[rows, :]], 0)
        chosen = dot(both, onehot).astype(BF16)
        sel_out[rows, :picked] = chosen[:HEAD_SIZE]
        sel_out[rows, picked:] = chosen[HEAD_SIZE:]
        return carry

    lax.fori_loop(0, ATTENTION_HEADS, pick, 0, unroll=4)


def local_kernel(base, live, q, k, v, out):
    length = q.shape[1]
    chunk = length // 2
    parts = 4
    step = length // parts
    dead = lanes(length) + base[0] >= live[0]

    def one_head(head, carry):
        rows = head_rows(head)
        query = scaled_query(q[rows, :])
        key = masked_key(k[rows, :], dead).T
        value = counted_value(v[rows, :])
        scores = dot(key, query[:, :chunk])
        for index in range(length // chunk):
            here = scores
            if (index + 1) * chunk < length:
                scores = dot(key, query[:, (index + 1) * chunk : (index + 2) * chunk])
            peak = jnp.max(here, axis=0, keepdims=True)
            total = None
            for part in range(parts):
                cut = slice(part * step, (part + 1) * step)
                weights = jnp.exp2(here[cut] - peak).astype(BF16)
                piece = dot(value[:, cut], weights)
                total = piece if total is None else total + piece
            done = total[:HEAD_SIZE] / total[HEAD_SIZE : HEAD_SIZE + 1]
            out[rows, index * chunk : (index + 1) * chunk] = done.astype(BF16)
        return carry

    lax.fori_loop(0, ATTENTION_HEADS, one_head, 0)


def dilated_kernel(base, live, offsets, q, k, v, gathered, near, w_out, cot, branch, grad, attn):
    length = q.shape[1]
    picked = length // RATE
    shards = gathered.shape[0]
    width = 2 * picked
    position = lanes(length) + base[0]
    dead = position >= live[0]
    slot = lanes(shards * width)
    inside = slot % width
    key_position = slot // width * length + inside * RATE

    def attend(key, query, value):
        scores = dot(key, query, 0, 0)
        peak = jnp.max(scores, axis=0, keepdims=True)
        weights = jnp.exp2(scores - peak).astype(BF16)
        return peak, dot(value, weights)

    def one_head(head, carry):
        rows = head_rows(head)
        offset = offsets[head]
        onehot = selector(length, offset)
        query = dot(scaled_query(q[rows, :]), onehot).astype(BF16)
        local_max, local_sum = attend(masked_key(k[rows, :], dead), query, counted_value(v[rows, :]))
        both = jnp.concatenate([gathered[shard, rows, :] for shard in range(shards)], 1)
        key_dead = (inside >= picked) | (key_position + offset >= live[0])
        value = jnp.concatenate([both[:, picked:], both[:, :picked]], 1)
        far_max, far_sum = attend(masked_key(both, key_dead), query, counted_value(value))
        top = jnp.maximum(local_max, far_max)
        total = jnp.exp2(local_max - top) * local_sum + jnp.exp2(far_max - top) * far_sum
        chosen = (total[:HEAD_SIZE] / total[HEAD_SIZE : HEAD_SIZE + 1]).astype(BF16)
        spread = dot(chosen, onehot, 1, 1)
        is_picked = position[:1] % RATE == offset
        merged = jnp.where(is_picked, spread, near[rows, :].astype(F32))
        attn[rows, :] = jnp.where(dead[:1], 0.0, merged).astype(BF16)
        return carry

    lax.fori_loop(0, ATTENTION_HEADS, one_head, 0, unroll=2)
    grad[...] = dot(attn[...], cot[...]).astype(BF16).T
    branch[...] = dot(attn[...].T, w_out[...]).astype(BF16)


def params():
    return pltpu.CompilerParams(vmem_limit_bytes=60 << 20)


def body(tiles, tile_count, offsets, w_query, w_key, w_value, w_out, cotangent):
    inputs = tiles[0]
    length, width = inputs.shape
    assert length == SEG
    picked = length // RATE
    base = (lax.axis_index("seq") * length).astype(jnp.int32).reshape(1)
    half = jax.ShapeDtypeStruct((width, length), BF16)
    query, key, value, chosen = pl.pallas_call(
        project_kernel,
        out_shape=(half, half, half, jax.ShapeDtypeStruct((width, 2 * picked), BF16)),
        in_specs=[SMEM] + [VMEM] * 4,
        out_specs=(VMEM,) * 4,
        compiler_params=params(),
    )(offsets, inputs, w_query, w_key, w_value)
    gathered = lax.all_gather(chosen, "seq", axis=0)
    near = pl.pallas_call(
        local_kernel,
        out_shape=half,
        in_specs=[SMEM] * 2 + [VMEM] * 3,
        out_specs=VMEM,
        compiler_params=params(),
        cost_estimate=pl.CostEstimate(flops=2 * 10**10, bytes_accessed=6 * 10**6, transcendentals=2 * 10**7),
    )(base, tile_count, query, key, value)
    branch, grad = pl.pallas_call(
        dilated_kernel,
        out_shape=(
            jax.ShapeDtypeStruct((length, width), BF16),
            jax.ShapeDtypeStruct((width, width), BF16),
        ),
        in_specs=[SMEM] * 3 + [VMEM] * 7,
        out_specs=(VMEM,) * 2,
        scratch_shapes=[pltpu.VMEM((width, length), BF16)],
        compiler_params=params(),
    )(base, tile_count, offsets, query, key, value, gathered, near, w_out, cotangent[0])
    share = lax.psum_scatter(grad, "seq", scatter_dimension=0, tiled=True)
    grad_part = lax.psum(share, "dp").astype(F32).T
    return (branch[None], grad_part)


def solution(mesh):
    in_specs = (P("dp", "seq", None), P("dp"), P(), P(), P(), P(), P(), P("dp", "seq", None))
    out_specs = (P("dp", "seq", None), P(None, "seq"))
    return jax.shard_map(body, mesh=mesh, in_specs=in_specs, out_specs=out_specs, check_vma=False)
```

time: 292 us -> 161 us (0.55)
  local copies, waits for them, and re-layouts: 79 us -> 0 us
  Pallas kernels: 0 us -> 65 us
  matrix products: 53.2 us -> 0 us
  other arithmetic: 39.2 us -> 1.64 us
  blocking collectives: 35 us -> 0 us
  waiting for transfers between devices: 62.4 us -> 79.5 us
  loops' own time: 6.89 us -> 0 us
    pallas_call x0 -> x3, Pallas kernels: none -> 65 us  [the longest x1 27.6 us: body(): pl.pallas_call(dilated_kernel, out_shape=(jax.ShapeDtypeStruct((length, w...]
    dot_general x15 -> x0, matrix products: 53.2 us -> none  [the longest x4 22.5 us: one_group(): jnp.einsum('shqk,skhd->sqhd', weights.astype(jnp.bfloat16), value_part, p...]
    reduce_scatter x0 -> x1, waiting for transfers between devices: none -> 35.8 us  [body(): share = lax.psum_scatter(grad, 'seq', scatter_dimension=0, tiled=True)]
    all_gather x2 -> x0, blocking collectives: 35 us -> none  [the longest x1 18.4 us: body(): lax.all_gather(key_sel.reshape(picked, D), 'seq', axis=0, tiled=True)]
    broadcast_in_dim x10 -> x0, local copies, waits for them, and re-layouts: 29.3 us -> none  [the longest x4 23 us: combine(): jnp.where(dilation_match[None, :, :, None], dilated_row_sum[:, None], 0.0)]
    unnamed x3, waiting for transfers between devices: 23.1 us -> 0.05 us
    another operation x3 -> x0, local copies, waits for them, and re-layouts: 21.5 us -> none  [select_rows(): tensor.reshape(segment_height // RATE, RATE, ATTENTION_HEADS, HEAD_SIZE)]
    reduce_sum x5 -> x0, other arithmetic: 17.7 us -> none  [the longest x4 16.4 us: one_group(): totals = jnp.sum(weights, axis=-1)]
  transfers between devices with their start and end apart: 2 -> 3, of which waited for: 2 -> 2; matrix products, arithmetic and copies ran while one was open for 7% -> 0% of each run, Pallas kernels for 0% -> 17%
where the time goes in v1:
time: 161 us
  waiting for transfers between devices  79.5 us (49%)
  Pallas kernels  65 us (40%)
  between operations  14.4 us (9%)
  other arithmetic  1.64 us (1%)
    psum x1, waiting for transfers between devices, body(): grad_part = lax.psum(share, 'dp').astype(F32).T  43.6 us
    reduce_scatter x1, waiting for transfers between devices, body(): share = lax.psum_scatter(grad, 'seq', scatter_dimension=0, tiled=True)  35.8 us
    pallas_call x1, Pallas kernels, body(): pl.pallas_call(dilated_kernel, out_shape=(jax.ShapeDtypeStruct((length, w...  27.6 us
    pallas_call x1, Pallas kernels, body(): pl.pallas_call(local_kernel, out_shape=half, in_specs=[SMEM] * 2 + [VMEM]...  27.4 us
    pallas_call x1, Pallas kernels, body(): pl.pallas_call(project_kernel, out_shape=(half, half, half, jax.ShapeDtyp...  10 us
  transfers between devices with their start and end apart: 3, of which 2 were waited for; matrix products, arithmetic and copies ran while one was open for 0% of the time, Pallas kernels for 17%

profile of v1, /device:TPU:0, one launch (start us, length us, event | category | flops | bytes accessed | tf_op | source)
XLA Modules:
  0.0 160.7 jit_solution(3754160205603540796)
XLA Ops:
  7.2 0.0 all-gather.3.cloned.1.call-start
  7.2 10.0 %shard_map.95 = (bf16[768,1024]{1,0:T(8,128)(2,1)}, bf16[768,1024]{1,0:T(8,128)(2,1)}, bf16[768,1024]{1,0:T(8,128)(2,1)}, bf16[768,128]{1,0:T(8,128)(2,1)}) custom-call(s32[16]{0:T(128)} %offsets.3, bf16[1024,768]{1,0:T(8,128)(2,1)} %bitcast.6, bf16[768,768]{1,0:T(8,128)(2,1)} %wq.1, bf16[768,768]{1,0:T(8,128)(2,1)} %wk.1, bf16[768,768]{1,0:T(8,128)(2,1)} %wv.1), custom_call_target="tpu_custom_call" | custom-call | tf_op jit(solution)/shard_map/pallas_call | solution.py:161
  17.2 0.0 all-gather.3.cloned.1.call-update
  17.3 0.0 reduce-scatter.2.cloned.1.call-start
  18.0 27.4 %shard_map.96.near = bf16[768,1024]{1,0:T(8,128)(2,1)} custom-call(s32[1]{0:T(128)} %bitcast.base, s32[1]{0:T(128)S(6)} %copy.11.live, bf16[768,1024]{1,0:T(8,128)(2,1)} %get-tuple-element.8.q, bf16[768,1024]{1,0:T(8,128)(2,1)} %get-tuple-element.9.k, bf16[768,1024]{1,0:T(8,128)(2,1)} %get-tuple-element.10.v), custom_call_target="tpu_custom_call" | custom-call | flops 20000000000 | bytes 6000000 | tf_op jit(solution)/shard_map/pallas_call | solution.py:169
  45.4 0.0 all-gather.3.cloned.1.call-done
  45.4 27.6 %shard_map.97 = (bf16[1024,768]{1,0:T(8,128)(2,1)}, bf16[768,768]{1,0:T(8,128)(2,1)}) custom-call(s32[1]{0:T(128)} %bitcast.base, s32[1]{0:T(128)S(6)} %copy.11.live, s32[16]{0:T(128)} %offsets.3, bf16[768,1024]{1,0:T(8,128)(2,1)} %get-tuple-element.8.q, bf16[768,1024]{1,0:T(8,128)(2,1)} %get-tuple-element.9.k, bf16[768,1024]{1,0:T(8,128)(2,1)} %get-tuple-element.10.v, ...), custom_call_target="tpu_custom_call" | custom-call | tf_op jit(solution)/shard_map/pallas_call | solution.py:177
  73.0 0.0 reduce-scatter.2.cloned.1.call-update
  73.0 0.0 all-reduce.2.cloned.1.call-start
  73.1 35.8 %reduce-scatter.2.cloned.1.call-done = bf16[96,768]{1,0:T(8,128)(2,1)} async-done(((bf16[768,768]{1,0:T(8,128)(2,1)}), bf16[96,768]{1,0:T(8,128)(2,1)}) %reduce-scatter.2.cloned.1.call-update) | async-done | bytes 147472 | tf_op jit(solution)/shard_map/reduce_scatter | solution.py:188
  108.8 0.0 all-reduce.2.cloned.1.call-update
  108.9 43.6 %all-reduce.2.cloned.1.call-done = bf16[768,96]{0,1:T(8,128)(2,1)} async-done(((bf16[768,96]{0,1:T(8,128)(2,1)}), bf16[768,96]{0,1:T(8,128)(2,1)}) %all-reduce.2.cloned.1.call-update) | async-done | bytes 147472 | tf_op jit(solution)/shard_map/psum | solution.py:189
  152.5 1.6 %transpose.7 = f32[768,96]{0,1:T(8,128)} convert(bf16[768,96]{0,1:T(8,128)(2,1)} %all-reduce.2.cloned.1.call-done) | non-fusion elementwise | flops 73728 | bytes 442368 | tf_op jit(solution)/shard_map/transpose | solution.py:189
Async XLA Ops:
  7.2 38.2 %all-gather.3.cloned.1.call-start = ((), (), s32[]{:S(2)}) async-start(), calls=%async_computation.3 | async-start | bytes 1769472 | tf_op jit(solution)/shard_map/all_gather | solution.py:168
  17.3 91.6 %reduce-scatter.2.cloned.1.call-start = ((), (), s32[]{:S(2)}) async-start(), calls=%async_computation.1 | async-start | bytes 1327104 | tf_op jit(solution)/shard_map/reduce_scatter | solution.py:188
  73.0 79.5 %all-reduce.2.cloned.1.call-start = ((), (), s32[]{:S(2)}) async-start(), calls=%async_computation.2 | async-start | bytes 294912 | tf_op jit(solution)/shard_map/psum | solution.py:189
Sparse Core Ops, SparseCore 0:
  17.4 27.9 all-gather.2
  73.1 35.6 reduce-scatter.1
  111.8 40.6 all-reduce.1

commit v2 on v1

--- a/solution.py
+++ b/solution.py
@@ -14,6 +14,8 @@
 NEGATIVE_FLOOR = -1e30
 LOG2_SCALE = 1.4426950408889634 / HEAD_SIZE**0.5
 PAD = 16
+LANES = 128
+MESH = pl.DeviceIdType.MESH
 BF16 = jnp.bfloat16
 F32 = jnp.float32
 VMEM = pl.BlockSpec(memory_space=pltpu.VMEM)
@@ -147,11 +149,135 @@
     branch[...] = dot(attn[...].T, w_out[...]).astype(BF16)
 
 
+def reduce_kernel(shards, slides, grad, out, stage, pair_in, chip, slide_in, chip_sum, line_in, final, *sems):
+    pair_send, pair_recv, slide_send, slide_recv, line_send, line_recv, last_send, last_recv = sems
+    me = lax.axis_index("seq")
+    slide = lax.axis_index("dp")
+    spots = shards // 2
+    spot, core = me // 2, me % 2
+    block = grad.shape[0] // shards
+    tiles = grad.shape[1] // LANES
+    part = block * tiles // slides
+    ahead = [lax.rem(spot + k, spots) for k in range(spots)]
+    others = [lax.rem(slide + k, slides) for k in range(slides)]
+    partner = {"seq": me + 1 - 2 * core}
+
+    barrier = pltpu.get_barrier_semaphore()
+    peers = [partner]
+    peers += [{"dp": others[k]} for k in range(1, slides)]
+    peers += [{"seq": 2 * ahead[k] + core} for k in range(1, spots)]
+    for peer in peers:
+        pl.semaphore_signal(barrier, inc=1, device_id=peer, device_id_type=MESH)
+    for shard in range(shards):
+        for tile in range(tiles):
+            stage[shard % 2, shard // 2, tile * block : (tile + 1) * block, :] = grad[
+                shard * block : (shard + 1) * block, tile * LANES : (tile + 1) * LANES
+            ]
+    pl.semaphore_wait(barrier, len(peers))
+
+    def copy(src, dst, send, recv, peer):
+        item = pltpu.make_async_remote_copy(
+            src_ref=src, dst_ref=dst, send_sem=send, recv_sem=recv, device_id=peer, device_id_type=MESH
+        )
+        item.start()
+        return item
+
+    turns = list(range(1, spots)) + [0]
+    pair = {
+        k: copy(stage.at[1 - core, ahead[k]], pair_in.at[k], pair_send.at[k], pair_recv.at[k], partner)
+        for k in turns
+    }
+    across = {}
+    for k in turns:
+        pair[k].wait_recv()
+        for p in range(slides):
+            rows = slice(p * part, (p + 1) * part)
+            mine = stage[core, ahead[k], rows, :].astype(F32) + pair_in[k, rows, :].astype(F32)
+            chip[k, p] = mine.astype(BF16)
+        for j in range(1, slides):
+            across[k, j] = copy(
+                chip.at[k, others[j]],
+                slide_in.at[k, j - 1],
+                slide_send.at[k, j - 1],
+                slide_recv.at[k, j - 1],
+                {"dp": others[j]},
+            )
+    along = {}
+    for k in turns:
+        total = chip[k, slide].astype(F32)
+        for j in range(1, slides):
+            across[k, j].wait_recv()
+            total = total + slide_in[k, j - 1].astype(F32)
+        chip_sum[k] = total.astype(BF16)
+        if k:
+            along[k] = copy(
+                chip_sum.at[k],
+                line_in.at[k - 1],
+                line_send.at[k - 1],
+                line_recv.at[k - 1],
+                {"seq": 2 * ahead[k] + core},
+            )
+    total = chip_sum[0].astype(F32)
+    for k in range(1, spots):
+        along[k].wait_recv()
+        total = total + line_in[k - 1].astype(F32)
+    own = pl.ds(pl.multiple_of(slide * part, PAD), part)
+    final[own, :] = total.astype(BF16)
+    last = [
+        copy(final.at[own, :], final.at[own, :], last_send.at[j - 1], last_recv.at[j - 1], {"dp": others[j]})
+        for j in range(1, slides)
+    ]
+    for item in last:
+        item.wait_recv()
+    for item in list(pair.values()) + list(across.values()) + list(along.values()) + last:
+        item.wait_send()
+    for tile in range(tiles):
+        out[tile * LANES : (tile + 1) * LANES, :] = final[tile * block : (tile + 1) * block, :].astype(F32).T
+
+
+def reduce_gradient(grad, shards, slides):
+    width = grad.shape[0]
+    block = width // shards
+    rows = block * (grad.shape[1] // LANES)
+    if block % PAD or rows % (slides * PAD) or shards % 2 or shards < 4 or slides < 2:
+        share = lax.psum_scatter(grad, "seq", scatter_dimension=0, tiled=True)
+        return lax.psum(share, "dp").astype(F32).T
+    spots = shards // 2
+    part = rows // slides
+    dma = pltpu.SemaphoreType.DMA
+    return pl.pallas_call(
+        functools.partial(reduce_kernel, shards, slides),
+        out_shape=jax.ShapeDtypeStruct((grad.shape[1], block), F32),
+        in_specs=[VMEM],
+        out_specs=VMEM,
+        scratch_shapes=[
+            pltpu.VMEM((2, spots, rows, LANES), BF16),
+            pltpu.VMEM((spots, rows, LANES), BF16),
+            pltpu.VMEM((spots, slides, part, LANES), BF16),
+            pltpu.VMEM((spots, slides - 1, part, LANES), BF16),
+            pltpu.VMEM((spots, part, LANES), BF16),
+            pltpu.VMEM((spots - 1, part, LANES), BF16),
+            pltpu.VMEM((rows, LANES), BF16),
+            dma((spots,)),
+            dma((spots,)),
+            dma((spots, slides - 1)),
+            dma((spots, slides - 1)),
+            dma((spots - 1,)),
+            dma((spots - 1,)),
+            dma((slides - 1,)),
+            dma((slides - 1,)),
+        ],
+        compiler_params=pltpu.CompilerParams(
+            vmem_limit_bytes=60 << 20, collective_id=0, has_side_effects=True
+        ),
+    )(grad)
+
+
 def params():
     return pltpu.CompilerParams(vmem_limit_bytes=60 << 20)
 
 
-def body(tiles, tile_count, offsets, w_query, w_key, w_value, w_out, cotangent):
+def body(shards, slides, tiles, tile_count, offsets, w_query, w_key, w_value, w_out, cotangent):
     inputs = tiles[0]
     length, width = inputs.shape
     assert length == SEG
@@ -185,12 +311,11 @@
         scratch_shapes=[pltpu.VMEM((width, length), BF16)],
         compiler_params=params(),
     )(base, tile_count, offsets, query, key, value, gathered, near, w_out, cotangent[0])
-    share = lax.psum_scatter(grad, "seq", scatter_dimension=0, tiled=True)
-    grad_part = lax.psum(share, "dp").astype(F32).T
-    return (branch[None], grad_part)
+    return (branch[None], reduce_gradient(grad, shards, slides))
 
 
 def solution(mesh):
     in_specs = (P("dp", "seq", None), P("dp"), P(), P(), P(), P(), P(), P("dp", "seq", None))
     out_specs = (P("dp", "seq", None), P(None, "seq"))
-    return jax.shard_map(body, mesh=mesh, in_specs=in_specs, out_specs=out_specs, check_vma=False)
+    run = functools.partial(body, mesh.shape["seq"], mesh.shape["dp"])
+    return jax.shard_map(run, mesh=mesh, in_specs=in_specs, out_specs=out_specs, check_vma=False)

time: 161 us -> 104 us (0.65)
  waiting for transfers between devices: 79.5 us -> 0.12 us
  Pallas kernels: 65 us -> 87.4 us
  local copies, waits for them, and re-layouts: 0 us -> 1.87 us
  other arithmetic: 1.64 us -> 0 us
    psum x1 -> x0, waiting for transfers between devices: 43.6 us -> none  [body(): grad_part = lax.psum(share, 'dp').astype(F32).T]
    reduce_scatter x1 -> x0, waiting for transfers between devices: 35.8 us -> none  [body(): share = lax.psum_scatter(grad, 'seq', scatter_dimension=0, tiled=True)]
    pallas_call x0 -> x1, Pallas kernels: none -> 22.4 us  [reduce_gradient(): pl.pallas_call(functools.partial(reduce_kernel, shards, slides), out_shap...]
    unnamed x0 -> x1, local copies, waits for them, and re-layouts: none -> 1.87 us
    transpose x1 -> x0, other arithmetic: 1.64 us -> none  [body(): grad_part = lax.psum(share, 'dp').astype(F32).T]
  transfers between devices with their start and end apart: 3 -> 1, of which waited for: 2 -> 1; matrix products, arithmetic and copies ran while one was open for 0% -> 0% of each run, Pallas kernels for 17% -> 26%
where the time goes in v2:
time: 104 us
  Pallas kernels  87.4 us (84%)
  between operations  14.7 us (14%)
  local copies, waits for them, and re-layouts  1.87 us (2%)
    pallas_call x1, Pallas kernels, body(): pl.pallas_call(dilated_kernel, out_shape=(jax.ShapeDtypeStruct((length, w...  27.6 us
    pallas_call x1, Pallas kernels, body(): pl.pallas_call(local_kernel, out_shape=half, in_specs=[SMEM] * 2 + [VMEM]...  27.4 us
    pallas_call x1, Pallas kernels, reduce_gradient(): pl.pallas_call(functools.partial(reduce_kernel, shards, slides), out_shap...  22.4 us
    pallas_call x1, Pallas kernels, body(): pl.pallas_call(project_kernel, out_shape=(half, half, half, jax.ShapeDtyp...  10 us
  transfers between devices with their start and end apart: 1, of which 1 were waited for; matrix products, arithmetic and copies ran while one was open for 0% of the time, Pallas kernels for 26%

profile of v2, /device:TPU:0, one launch (start us, length us, event | category | flops | bytes accessed | tf_op | source)
XLA Modules:
  0.0 104.1 jit_solution(12797355441805437408)
XLA Ops:
  7.2 0.0 all-gather.3.cloned.1.call-start
  7.2 10.0 %shard_map.95 = (bf16[768,1024]{1,0:T(8,128)(2,1)}, bf16[768,1024]{1,0:T(8,128)(2,1)}, bf16[768,1024]{1,0:T(8,128)(2,1)}, bf16[768,128]{1,0:T(8,128)(2,1)}) custom-call(s32[16]{0:T(128)} %offsets.3, bf16[1024,768]{1,0:T(8,128)(2,1)} %bitcast.5, bf16[768,768]{1,0:T(8,128)(2,1)} %wq.1, bf16[768,768]{1,0:T(8,128)(2,1)} %wk.1, bf16[768,768]{1,0:T(8,128)(2,1)} %wv.1), custom_call_target="tpu_custom_call" | custom-call | tf_op jit(solution)/shard_map/pallas_call | solution.py:287
  17.2 0.0 all-gather.3.cloned.1.call-update
  17.9 27.4 %shard_map.96.near = bf16[768,1024]{1,0:T(8,128)(2,1)} custom-call(s32[1]{0:T(128)} %bitcast.base, s32[1]{0:T(128)S(6)} %copy.11.live, bf16[768,1024]{1,0:T(8,128)(2,1)} %get-tuple-element.8.q, bf16[768,1024]{1,0:T(8,128)(2,1)} %get-tuple-element.9.k, bf16[768,1024]{1,0:T(8,128)(2,1)} %get-tuple-element.10.v), custom_call_target="tpu_custom_call" | custom-call | flops 20000000000 | bytes 6000000 | tf_op jit(solution)/shard_map/pallas_call | solution.py:295
  45.3 0.1 all-gather.3.cloned.1.call-done
  45.4 27.6 %shard_map.97 = (bf16[1024,768]{1,0:T(8,128)(2,1)}, bf16[768,768]{1,0:T(8,128)(2,1)}) custom-call(s32[1]{0:T(128)} %bitcast.base, s32[1]{0:T(128)S(6)} %copy.11.live, s32[16]{0:T(128)} %offsets.3, bf16[768,1024]{1,0:T(8,128)(2,1)} %get-tuple-element.8.q, bf16[768,1024]{1,0:T(8,128)(2,1)} %get-tuple-element.9.k, bf16[768,1024]{1,0:T(8,128)(2,1)} %get-tuple-element.10.v, ...), custom_call_target="tpu_custom_call" | custom-call | tf_op jit(solution)/shard_map/pallas_call | solution.py:303
  73.0 22.4 %shard_map.98 = f32[768,96]{1,0:T(8,128)} custom-call(bf16[768,768]{1,0:T(8,128)(2,1)} %get-tuple-element.13.grad), custom_call_target="tpu_custom_call" | custom-call | tf_op jit(solution)/shard_map/pallas_call | solution.py:248
  95.4 1.9 %copy.10 = f32[768,96]{0,1:T(8,128)} copy(f32[768,96]{1,0:T(8,128)} %shard_map.98) | data formatting | bytes 589824
Async XLA Ops:
  7.2 38.3 %all-gather.3.cloned.1.call-start = ((), (), s32[]{:S(2)}) async-start(), calls=%async_computation | async-start | bytes 1769472 | tf_op jit(solution)/shard_map/all_gather | solution.py:294
Sparse Core Ops, SparseCore 0:
  17.4 27.9 all-gather.2

commit v3 on v1

v3 whole, which is shorter than its diff:
```python
import functools

import jax
import jax.numpy as jnp
from jax import lax
from jax.experimental import pallas as pl
from jax.experimental.pallas import tpu as pltpu
from jax.sharding import PartitionSpec as P

ATTENTION_HEADS = 16
HEAD_SIZE = 48
SEG = 1024
RATE = 16
NEGATIVE_FLOOR = -1e30
LOG2_SCALE = 1.4426950408889634 / HEAD_SIZE**0.5
PAD = 16
LANES = 128
MESH = pl.DeviceIdType.MESH
BF16 = jnp.bfloat16
F32 = jnp.float32
VMEM = pl.BlockSpec(memory_space=pltpu.VMEM)
SMEM = pl.BlockSpec(memory_space=pltpu.SMEM)


def dot(a, b, ca=1, cb=0):
    return lax.dot_general(a, b, (((ca,), (cb,)), ((), ())), preferred_element_type=F32)


def head_rows(head):
    return pl.ds(pl.multiple_of(head * HEAD_SIZE, PAD), HEAD_SIZE)


def scaled_query(query):
    scaled = query.astype(F32) * LOG2_SCALE
    high = scaled.astype(BF16)
    low = (scaled - high.astype(F32)).astype(BF16)
    return jnp.concatenate([high, low, jnp.ones((PAD, query.shape[1]), BF16)], 0)


def masked_key(key, dead):
    row = lax.broadcasted_iota(jnp.int32, (PAD, key.shape[1]), 0)
    mask = jnp.where(dead & (row == 0), NEGATIVE_FLOOR, 0.0).astype(BF16)
    return jnp.concatenate([key, key, mask], 0)


def counted_value(value):
    return jnp.concatenate([value, jnp.ones((PAD, value.shape[1]), BF16)], 0)


def lanes(width):
    return lax.broadcasted_iota(jnp.int32, (PAD, width), 1)


def selector(length, offset):
    shape = (length, length // RATE)
    token = lax.broadcasted_iota(jnp.int32, shape, 0)
    pick = lax.broadcasted_iota(jnp.int32, shape, 1)
    return jnp.where(token == RATE * pick + offset, 1.0, 0.0).astype(BF16)


def attention_kernel(
    shards, slides, fused, live, offsets, x, wq, wk, wv, w_out, cot, branch, grad, q, k, v, near, attn, chosen,
    gathered, gather_send, gather_recv, *scratch
):
    width, length = q.shape
    picked = length // RATE
    block = 2 * picked
    half = ATTENTION_HEADS // 2
    me = lax.axis_index("seq")
    slide = lax.axis_index("dp")
    spots = shards // 2
    spot, core = me // 2, me % 2
    ahead = [lax.rem(spot + n, spots) for n in range(spots)]
    others = [lax.rem(slide + n, slides) for n in range(slides)]
    partner = {"seq": me + 1 - 2 * core}
    line = [{"seq": 2 * ahead[n] + core} for n in range(spots)]
    peers = [partner] + line[1:]
    if fused:
        peers = peers + [{"dp": others[n]} for n in range(1, slides)]
    barrier = pltpu.get_barrier_semaphore()
    for peer in peers:
        pl.semaphore_signal(barrier, inc=1, device_id=peer, device_id_type=MESH)

    def copy(src, dst, send, recv, peer):
        item = pltpu.make_async_remote_copy(
            src_ref=src, dst_ref=dst, send_sem=send, recv_sem=recv, device_id=peer, device_id_type=MESH
        )
        item.start()
        return item

    tiles = x[...]
    for weight, out in ((wk, k), (wv, v)):
        out[...] = dot(weight[...].T, tiles, 1, 1).astype(BF16)

    def pick(head, carry):
        rows = head_rows(head)
        onehot = selector(length, offsets[head])
        both = jnp.concatenate([k[rows, :], v[rows, :]], 0)
        part = dot(both, onehot).astype(BF16)
        chosen[rows, :picked] = part[:HEAD_SIZE]
        chosen[rows, picked:] = part[HEAD_SIZE:]
        return carry

    lax.fori_loop(0, ATTENTION_HEADS, pick, 0, unroll=4)
    pl.semaphore_wait(barrier, len(peers))
    pending = []
    for n in range(1, spots):
        pending.append(copy(chosen, gathered.at[0, n], gather_send.at[0, n], gather_recv.at[0, n], line[n]))
    pending.append(copy(chosen, gathered.at[1, 0], gather_send.at[1, 0], gather_recv.at[1, 0], partner))
    gathered[0, 0] = chosen[...]
    q[...] = dot(wq[...].T, tiles, 1, 1).astype(BF16)

    position = lanes(length) + me * length
    dead = position >= live[0]
    inside = lanes(block)

    def local(head):
        chunk = length // 2
        parts = 4
        step = length // parts
        rows = head_rows(head)
        query = scaled_query(q[rows, :])
        key = masked_key(k[rows, :], dead).T
        value = counted_value(v[rows, :])
        scores = dot(key, query[:, :chunk])
        for index in range(length // chunk):
            here = scores
            if (index + 1) * chunk < length:
                scores = dot(key, query[:, (index + 1) * chunk : (index + 2) * chunk])
            peak = jnp.max(here, axis=0, keepdims=True)
            total = None
            for part in range(parts):
                cut = slice(part * step, (part + 1) * step)
                weights = jnp.exp2(here[cut] - peak).astype(BF16)
                piece = dot(value[:, cut], weights)
                total = piece if total is None else total + piece
            done = total[:HEAD_SIZE] / total[HEAD_SIZE : HEAD_SIZE + 1]
            near[rows, index * chunk : (index + 1) * chunk] = done.astype(BF16)

    def attend(key, query, value):
        scores = dot(key, query, 0, 0)
        peak = jnp.max(scores, axis=0, keepdims=True)
        weights = jnp.exp2(scores - peak).astype(BF16)
        return peak, dot(value, weights)

    def dilated(head):
        rows = head_rows(head)
        offset = offsets[head]
        onehot = selector(length, offset)
        query = dot(scaled_query(q[rows, :]), onehot).astype(BF16)
        local_max, local_sum = attend(masked_key(k[rows, :], dead), query, counted_value(v[rows, :]))
        keys, gone = [], []
        for side in range(2):
            for n in range(spots):
                keys.append(gathered[side, n, rows, :])
                origin = 2 * lax.rem(spot - n + spots, spots) + lax.rem(core + side, 2)
                gone.append((inside >= picked) | (origin * length + inside * RATE + offset >= live[0]))
        both = jnp.concatenate(keys, 1)
        gone = jnp.concatenate([jnp.where(item, 1, 0) for item in gone], 1) == 1
        value = jnp.concatenate([both[:, picked:], both[:, :picked]], 1)
        far_max, far_sum = attend(masked_key(both, gone), query, counted_value(value))
        top = jnp.maximum(local_max, far_max)
        total = jnp.exp2(local_max - top) * local_sum + jnp.exp2(far_max - top) * far_sum
        part = (total[:HEAD_SIZE] / total[HEAD_SIZE : HEAD_SIZE + 1]).astype(BF16)
        spread = dot(part, onehot, 1, 1)
        is_picked = position[:1] % RATE == offset
        merged = jnp.where(is_picked, spread, near[rows, :].astype(F32))
        attn[rows, :] = jnp.where(dead[:1], 0.0, merged).astype(BF16)

    def first(head, carry):
        local(head)
        return carry

    def second(head, carry):
        dilated(head)
        local(head + half)
        return carry

    def third(pair, carry):
        dilated(2 * pair)
        dilated(2 * pair + 1)
        return carry

    lax.fori_loop(0, half, first, 0)
    for n in range(1, spots):
        pending[n - 1].wait_recv()
        pending.append(
            copy(gathered.at[0, n], gathered.at[1, n], gather_send.at[1, n], gather_recv.at[1, n], partner)
        )
    for item in pending[spots - 1 :]:
        item.wait_recv()
    lax.fori_loop(0, half, second, 0)

    def gradient(rows):
        return dot(attn[rows, :], cot[...]).astype(BF16).T

    if not fused:
        lax.fori_loop(half // 2, half, third, 0)
        grad[...] = gradient(slice(0, width))
        branch[...] = dot(attn[...].T, w_out[...]).astype(BF16)
        for item in pending:
            item.wait_send()
        return

    stage, pair_in, chip, slide_in, chip_sum, line_in, final = scratch[:7]
    pair_send, pair_recv, slide_send, slide_recv, line_send, line_recv, last_send, last_recv = scratch[7:]
    columns = width // shards
    wide = width // 2
    count = wide // LANES
    part = columns * count // slides
    turns = list(range(1, spots)) + [0]
    pair, across, along, last = {}, {}, {}, {}

    def open_pair(g):
        share = gradient(slice(g * wide, (g + 1) * wide))
        for shard in range(shards):
            for tile in range(count):
                stage[g, shard % 2, shard // 2, tile * columns : (tile + 1) * columns, :] = share[
                    shard * columns : (shard + 1) * columns, tile * LANES : (tile + 1) * LANES
                ]
        for n in turns:
            pair[g, n] = copy(
                stage.at[g, 1 - core, ahead[n]],
                pair_in.at[g, n],
                pair_send.at[g, n],
                pair_recv.at[g, n],
                partner,
            )

    def open_across(g):
        for n in turns:
            pair[g, n].wait_recv()
            mine = stage[g, core, ahead[n]].astype(F32) + pair_in[g, n].astype(F32)
            for p in range(slides):
                chip[g, n, p] = mine[p * part : (p + 1) * part].astype(BF16)
            for j in range(1, slides):
                across[g, n, j] = copy(
                    chip.at[g, n, others[j]],
                    slide_in.at[g, n, j - 1],
                    slide_send.at[g, n, j - 1],
                    slide_recv.at[g, n, j - 1],
                    {"dp": others[j]},
                )

    def open_along(g):
        for n in turns:
            total = chip[g, n, slide].astype(F32)
            for j in range(1, slides):
                across[g, n, j].wait_recv()
                total = total + slide_in[g, n, j - 1].astype(F32)
            chip_sum[g, n] = total.astype(BF16)
            if n:
                along[g, n] = copy(
                    chip_sum.at[g, n],
                    line_in.at[g, n - 1],
                    line_send.at[g, n - 1],
                    line_recv.at[g, n - 1],
                    line[n],
                )

    def open_last(g):
        total = chip_sum[g, 0].astype(F32)
        for n in range(1, spots):
            along[g, n].wait_recv()
            total = total + line_in[g, n - 1].astype(F32)
        final[g, slide] = total.astype(BF16)
        for j in range(1, slides):
            last[g, j] = copy(
                final.at[g, slide],
                final.at[g, slide],
                last_send.at[g, j - 1],
                last_recv.at[g, j - 1],
                {"dp": others[j]},
            )

    def close(g):
        for j in range(1, slides):
            last[g, j].wait_recv()
        full = jnp.concatenate([final[g, p].astype(F32) for p in range(slides)], 0)
        for tile in range(count):
            rows = slice(g * wide + tile * LANES, g * wide + (tile + 1) * LANES)
            grad[rows, :] = full[tile * columns : (tile + 1) * columns].T

    open_pair(0)
    lax.fori_loop(half // 2, half // 2 + half // 4, third, 0)
    open_across(0)
    lax.fori_loop(half // 2 + half // 4, half, third, 0)
    open_along(0)
    open_pair(1)
    open_last(0)
    open_across(1)
    branch[...] = dot(attn[...].T, w_out[...]).astype(BF16)
    open_along(1)
    close(0)
    open_last(1)
    close(1)
    for group in (pending, pair.values(), across.values(), along.values(), last.values()):
        for item in group:
            item.wait_send()


def body(shards, slides, tiles, tile_count, offsets, w_query, w_key, w_value, w_out, cotangent):
    inputs = tiles[0]
    length, width = inputs.shape
    assert length == SEG and shards % 2 == 0
    spots = shards // 2
    columns = width // shards
    rows = columns * (width // 2 // LANES)
    fused = columns % PAD == 0 and rows % (8 * slides) == 0 and spots > 1 and slides > 1
    dma = pltpu.SemaphoreType.DMA
    held = pltpu.VMEM((width, length), BF16)
    block = 2 * (length // RATE)
    scratch = [held] * 5 + [
        pltpu.VMEM((width, block), BF16),
        pltpu.VMEM((2, spots, width, block), BF16),
        dma((2, spots)),
        dma((2, spots)),
    ]
    grad_type = jax.ShapeDtypeStruct((width, width), BF16)
    if fused:
        part = rows // slides
        grad_type = jax.ShapeDtypeStruct((width, columns), F32)
        scratch += [
            pltpu.VMEM((2, 2, spots, rows, LANES), BF16),
            pltpu.VMEM((2, spots, rows, LANES), BF16),
            pltpu.VMEM((2, spots, slides, part, LANES), BF16),
            pltpu.VMEM((2, spots, slides - 1, part, LANES), BF16),
            pltpu.VMEM((2, spots, part, LANES), BF16),
            pltpu.VMEM((2, spots - 1, part, LANES), BF16),
            pltpu.VMEM((2, slides, part, LANES), BF16),
        ]
        for shape in ((2, spots), (2, spots, slides - 1), (2, spots - 1), (2, slides - 1)):
            scratch += [dma(shape), dma(shape)]
    branch, grad = pl.pallas_call(
        functools.partial(attention_kernel, shards, slides, fused),
        out_shape=(jax.ShapeDtypeStruct((length, width), BF16), grad_type),
        in_specs=[SMEM] * 2 + [VMEM] * 6,
        out_specs=(VMEM,) * 2,
        scratch_shapes=scratch,
        compiler_params=pltpu.CompilerParams(
            vmem_limit_bytes=60 << 20, collective_id=0, has_side_effects=True
        ),
    )(tile_count, offsets, inputs, w_query, w_key, w_value, w_out, cotangent[0])
    if not fused:
        share = lax.psum_scatter(grad, "seq", scatter_dimension=0, tiled=True)
        grad = lax.psum(share, "dp").astype(F32).T
    return (branch[None], grad)


def solution(mesh):
    in_specs = (P("dp", "seq", None), P("dp"), P(), P(), P(), P(), P(), P("dp", "seq", None))
    out_specs = (P("dp", "seq", None), P(None, "seq"))
    run = functools.partial(body, mesh.shape["seq"], mesh.shape["dp"])
    return jax.shard_map(run, mesh=mesh, in_specs=in_specs, out_specs=out_specs, check_vma=False)
```

time: 161 us -> 85.5 us (0.53)
  waiting for transfers between devices: 79.5 us -> 0 us
  Pallas kernels: 65 us -> 79.5 us
  between operations: 14.4 us -> 1.29 us
  local copies, waits for them, and re-layouts: 0 us -> 4.52 us
  other arithmetic: 1.64 us -> 0 us
    psum x1 -> x0, waiting for transfers between devices: 43.6 us -> none  [body(): grad_part = lax.psum(share, 'dp').astype(F32).T]
    reduce_scatter x1 -> x0, waiting for transfers between devices: 35.8 us -> none  [body(): share = lax.psum_scatter(grad, 'seq', scatter_dimension=0, tiled=True)]
    pallas_call x3 -> x1, Pallas kernels: 65 us -> 79.5 us  [body(): pl.pallas_call(functools.partial(attention_kernel, shards, slides, fused)...]
    unnamed x0 -> x2, local copies, waits for them, and re-layouts: none -> 4.52 us
    transpose x1 -> x0, other arithmetic: 1.64 us -> none  [body(): grad_part = lax.psum(share, 'dp').astype(F32).T]
  transfers between devices with their start and end apart: 3 -> 0, of which waited for: 2 -> 0; matrix products, arithmetic and copies ran while one was open for 0% -> 0% of each run, Pallas kernels for 17% -> 0%
where the time goes in v3:
time: 85.5 us; the launch traced here: 85.3 us
  Pallas kernels  79.5 us (93%)
  local copies, waits for them, and re-layouts  4.52 us (5%)
  between operations  1.29 us (2%)
    pallas_call x1, Pallas kernels, body(): pl.pallas_call(functools.partial(attention_kernel, shards, slides, fused)...  79.5 us
    unnamed x2, local copies, waits for them, and re-layouts  4.52 us

profile of v3, /device:TPU:0, one launch (start us, length us, event | category | flops | bytes accessed | tf_op | source)
XLA Modules:
  0.0 85.3 jit_solution(15032341958147472165)
XLA Ops:
  1.3 79.5 %shard_map.95 = (bf16[1024,768]{1,0:T(8,128)(2,1)}, f32[768,96]{1,0:T(8,128)}) custom-call(s32[1]{0:T(128)S(6)} %copy.12.live, s32[16]{0:T(128)} %offsets.1, bf16[1024,768]{1,0:T(8,128)(2,1)} %bitcast.4, bf16[768,768]{1,0:T(8,128)(2,1)} %wq.1, bf16[768,768]{1,0:T(8,128)(2,1)} %wk.1, bf16[768,768]{1,0:T(8,128)(2,1)} %wv.1, bf16[768,768]{1,0:T(8,128)(2,1)} %w_out.1, ...), custom_call_target="tpu_custom_call" | custom-call | tf_op jit(solution)/shard_map/pallas_call | solution.py:334
  80.8 1.9 %copy.10 = f32[768,96]{0,1:T(8,128)} copy(f32[768,96]{1,0:T(8,128)} %get-tuple-element.7) | data formatting | bytes 589824
  82.6 2.7 %copy.13 = bf16[1,1024,768]{2,1,0:T(8,128)(2,1)} copy(bf16[1,1024,768]{2,1,0:T(8,128)(2,1)} %bitcast.3) | data formatting | bytes 3145728

commit v4 on v3

--- a/solution.py
+++ b/solution.py
@@ -66,6 +66,7 @@
     picked = length // RATE
     block = 2 * picked
     half = ATTENTION_HEADS // 2
+    lead = half + 2
     me = lax.axis_index("seq")
     slide = lax.axis_index("dp")
     spots = shards // 2
@@ -103,11 +104,67 @@
 
     lax.fori_loop(0, ATTENTION_HEADS, pick, 0, unroll=4)
     pl.semaphore_wait(barrier, len(peers))
-    pending = []
-    for n in range(1, spots):
-        pending.append(copy(chosen, gathered.at[0, n], gather_send.at[0, n], gather_recv.at[0, n], line[n]))
-    pending.append(copy(chosen, gathered.at[1, 0], gather_send.at[1, 0], gather_recv.at[1, 0], partner))
-    gathered[0, 0] = chosen[...]
+    def relay(src, origin, way):
+        slot = gathered.at[1 if way == 2 else 0, origin]
+        return pltpu.make_async_remote_copy(
+            src_ref=src,
+            dst_ref=slot,
+            send_sem=gather_send.at[way, origin],
+            recv_sem=gather_recv.at[1 if way == 2 else 0, origin],
+            device_id=({"seq": me + 2}, {"seq": me - 2}, partner)[way],
+            device_id_type=MESH,
+        )
+
+    @pl.when(spot < spots - 1)
+    def _():
+        relay(chosen, spot, 0).start()
+
+    @pl.when(spot > 0)
+    def _():
+        relay(chosen, spot, 1).start()
+
+    relay(chosen, spot, 2).start()
+    gathered[0, spot] = chosen[...]
+
+    def pass_on(step):
+        @pl.when(spot >= step)
+        def _():
+            origin = spot - step
+            slot = gathered.at[0, origin]
+            relay(slot, origin, 0).wait_recv()
+
+            @pl.when(spot < spots - 1)
+            def _():
+                relay(slot, origin, 0).start()
+
+            relay(slot, origin, 2).start()
+
+        @pl.when(spot + step < spots)
+        def _():
+            origin = spot + step
+            slot = gathered.at[0, origin]
+            relay(slot, origin, 1).wait_recv()
+
+            @pl.when(spot > 0)
+            def _():
+                relay(slot, origin, 1).start()
+
+            relay(slot, origin, 2).start()
+
+    def end_gather():
+        for origin in range(spots):
+            slot = gathered.at[0, origin]
+
+            @pl.when((spot >= origin) & (spot < spots - 1))
+            def _():
+                relay(slot, origin, 0).wait_send()
+
+            @pl.when((spot <= origin) & (spot > 0))
+            def _():
+                relay(slot, origin, 1).wait_send()
+
+            relay(slot, origin, 2).wait_send()
+
     q[...] = dot(wq[...].T, tiles, 1, 1).astype(BF16)
 
     position = lanes(length) + me * length
@@ -153,7 +210,7 @@
         for side in range(2):
             for n in range(spots):
                 keys.append(gathered[side, n, rows, :])
-                origin = 2 * lax.rem(spot - n + spots, spots) + lax.rem(core + side, 2)
+                origin = 2 * n + lax.rem(core + side, 2)
                 gone.append((inside >= picked) | (origin * length + inside * RATE + offset >= live[0]))
         both = jnp.concatenate(keys, 1)
         gone = jnp.concatenate([jnp.where(item, 1, 0) for item in gone], 1) == 1
@@ -173,7 +230,7 @@
 
     def second(head, carry):
         dilated(head)
-        local(head + half)
+        local(head + lead)
         return carry
 
     def third(pair, carry):
@@ -181,15 +238,15 @@
         dilated(2 * pair + 1)
         return carry
 
-    lax.fori_loop(0, half, first, 0)
-    for n in range(1, spots):
-        pending[n - 1].wait_recv()
-        pending.append(
-            copy(gathered.at[0, n], gathered.at[1, n], gather_send.at[1, n], gather_recv.at[1, n], partner)
-        )
-    for item in pending[spots - 1 :]:
-        item.wait_recv()
-    lax.fori_loop(0, half, second, 0)
+    cuts = [n * (lead - 1) // (spots - 1) for n in range(spots)]
+    for step in range(1, spots):
+        lax.fori_loop(cuts[step - 1], cuts[step], first, 0)
+        pass_on(step)
+    lax.fori_loop(cuts[-1], lead, first, 0)
+    for origin in range(spots):
+        relay(gathered.at[0, origin], origin, 2).wait_recv()
+    lax.fori_loop(0, ATTENTION_HEADS - lead, second, 0)
+    lax.fori_loop((ATTENTION_HEADS - lead) // 2, half // 2, third, 0)
 
     def gradient(rows):
         return dot(attn[rows, :], cot[...]).astype(BF16).T
@@ -198,8 +255,7 @@
         lax.fori_loop(half // 2, half, third, 0)
         grad[...] = gradient(slice(0, width))
         branch[...] = dot(attn[...].T, w_out[...]).astype(BF16)
-        for item in pending:
-            item.wait_send()
+        end_gather()
         return
 
     stage, pair_in, chip, slide_in, chip_sum, line_in, final = scratch[:7]
@@ -294,7 +350,8 @@
     close(0)
     open_last(1)
     close(1)
-    for group in (pending, pair.values(), across.values(), along.values(), last.values()):
+    end_gather()
+    for group in (pair.values(), across.values(), along.values(), last.values()):
         for item in group:
             item.wait_send()
 
@@ -313,7 +370,7 @@
     scratch = [held] * 5 + [
         pltpu.VMEM((width, block), BF16),
         pltpu.VMEM((2, spots, width, block), BF16),
-        dma((2, spots)),
+        dma((3, spots)),
         dma((2, spots)),
     ]
     grad_type = jax.ShapeDtypeStruct((width, width), BF16)

time: 85.5 us -> 81.8 us (0.957)
  Pallas kernels: 79.5 us -> 75.8 us
    pallas_call x1, Pallas kernels: 79.5 us -> 75.8 us  [body(): pl.pallas_call(functools.partial(attention_kernel, shards, slides, fused)...]
where the time goes in v4:
time: 81.8 us; the launch traced here: 81.6 us
  Pallas kernels  75.8 us (93%)
  local copies, waits for them, and re-layouts  4.52 us (6%)
  between operations  1.29 us (2%)
    pallas_call x1, Pallas kernels, body(): pl.pallas_call(functools.partial(attention_kernel, shards, slides, fused)...  75.8 us
    unnamed x2, local copies, waits for them, and re-layouts  4.52 us

profile of v4, /device:TPU:0, one launch (start us, length us, event | category | flops | bytes accessed | tf_op | source)
XLA Modules:
  0.0 81.6 jit_solution(7817652561286796545)
XLA Ops:
  1.3 75.8 %shard_map.95 = (bf16[1024,768]{1,0:T(8,128)(2,1)}, f32[768,96]{1,0:T(8,128)}) custom-call(s32[1]{0:T(128)S(6)} %copy.12.live, s32[16]{0:T(128)} %offsets.1, bf16[1024,768]{1,0:T(8,128)(2,1)} %bitcast.4, bf16[768,768]{1,0:T(8,128)(2,1)} %wq.1, bf16[768,768]{1,0:T(8,128)(2,1)} %wk.1, bf16[768,768]{1,0:T(8,128)(2,1)} %wv.1, bf16[768,768]{1,0:T(8,128)(2,1)} %w_out.1, ...), custom_call_target="tpu_custom_call" | custom-call | tf_op jit(solution)/shard_map/pallas_call | solution.py:391
  77.1 1.9 %copy.10 = f32[768,96]{0,1:T(8,128)} copy(f32[768,96]{1,0:T(8,128)} %get-tuple-element.7) | data formatting | bytes 589824
  79.0 2.7 %copy.13 = bf16[1,1024,768]{2,1,0:T(8,128)(2,1)} copy(bf16[1,1024,768]{2,1,0:T(8,128)(2,1)} %bitcast.3) | data formatting | bytes 3145728
